TPU v7x, 128 devices: a whole 4x4x4 slice. The times are simulated.
128 devices in a mesh: gx: 8 (over y, core), gy: 4 (over x), gz: 4 (over z).
Axes of the slice: x: 4, y: 4, z: 4, core: 2. Of those that a mesh axis runs over, the one named last changes fastest.
Arguments:
- pressure_source: float32 [128, 256, 1024], P('gx', 'gy', 'gz'), may hold values from -6 to 6
- cell_density: float32 [1024], P('gz'), may hold values from 0.3 to 3
- face_density: float32 [1024], P('gz'), may hold values from 0.3 to 3
Outputs:
- smoothed: float32 [128, 256, 1024], P('gx', 'gy', 'gz')
- coarse_solution: float32 [16, 32, 128], P('gx')
All inputs are finite; a program needn't handle non-finite values.
Results may differ from a plain program's by a relative error of at most 0.0001.
Values sent between devices are 32-bit elements; how exact they have to be, the bound alone decides.
A program may use at most 192 MiB of HBM per device.

v0:
```python
import jax
import jax.numpy as jnp
from jax import lax
from jax.sharding import PartitionSpec as P

LEVELS = 3
SWEEPS = 6
COARSE_SWEEPS = 8
damping = 0.8


def padded_2(block, sides, width):
    for axis, dim in sides:
        count = lax.axis_size(axis)
        forward = [(i, i + 1) for i in range(count - 1)]
        forward.append((count - 1, 0))
        backward = [(target, source) for source, target in forward]
        low = lax.ppermute(
            lax.slice_in_dim(block, block.shape[dim] - width, None, axis=dim), axis, forward
        )
        high = lax.ppermute(lax.slice_in_dim(block, 0, width, axis=dim), axis, backward)
        block = jnp.concatenate([low, block, high], axis=dim)
    return block


def passed_along(block, axis, distance):
    devices = range(lax.axis_size(axis))
    route = [((i - distance) % len(devices), i) for i in devices]
    return lax.ppermute(block, axis, route)


def from_behind(value, axis, steps):
    count = lax.axis_size(axis)
    leading, last = (max(0, -steps), min(count, count - steps))
    return lax.ppermute(value, axis, [(source, source + steps) for source in range(leading, last)])


def level_apply(iterate, centre_coef, below_coef, above_coef, bottom_flag):
    padded = padded_2(iterate, (("gx", 0), ("gy", 1), ("gz", 2)), 1)
    horizontal = (
        4.0 * iterate
        - padded[:-2, 1:-1, 1:-1]
        - padded[2:, 1:-1, 1:-1]
        - padded[1:-1, :-2, 1:-1]
        - padded[1:-1, 2:, 1:-1]
    )
    depth = iterate.shape[2]
    first_plane = lax.broadcasted_iota(jnp.int32, (1, 1, depth), 2) == 0
    beneath = jnp.where(first_plane & bottom_flag, 0.0, padded[1:-1, 1:-1, :-2])
    overhead = padded[1:-1, 1:-1, 2:]
    return (
        centre_coef * horizontal
        + below_coef * (iterate - beneath)
        + above_coef * (iterate - overhead)
    )


def slab_apply(iterate, centre_coef, below_coef, above_coef):
    from_west = passed_along(iterate[-1:], "gx", 1)
    from_east = passed_along(iterate[:1], "gx", -1)
    western = jnp.concatenate([from_west, iterate[:-1]], axis=0)
    eastern = jnp.concatenate([iterate[1:], from_east], axis=0)
    horizontal = (
        4.0 * iterate - western - eastern - jnp.roll(iterate, 1, 1) - jnp.roll(iterate, -1, 1)
    )
    zero_plane = jnp.zeros_like(iterate[:, :, :1])
    beneath = jnp.concatenate([zero_plane, iterate[:, :, :-1]], axis=2)
    overhead = jnp.concatenate([iterate[:, :, 1:], zero_plane], axis=2)
    return (
        centre_coef * horizontal
        + below_coef * (iterate - beneath)
        + above_coef * (iterate - overhead)
    )


def smooth_with(operator, source_term, centre_coef, below_coef, above_coef, sweep_count):
    inverse_diag = 1.0 / (4.0 * centre_coef + below_coef + above_coef)
    iterate = damping * source_term * inverse_diag
    for sweep_index in range(sweep_count - 1):
        iterate = iterate + damping * (source_term - operator(iterate)) * inverse_diag
    return iterate


def restrict(residual):
    extent = residual.shape
    blocks = residual.reshape(extent[0] // 2, 2, extent[1] // 2, 2, extent[2] // 2, 2)
    return 0.5 * jnp.sum(blocks, axis=(1, 3, 5))


def on_device(pressure_source, cell_density, face_density):
    bottom_flag = lax.axis_index("gz") == 0
    top_value = from_behind(face_density[:1], "gz", -1)
    centre_coef = cell_density
    below_coef = face_density
    above_coef = jnp.concatenate([face_density[1:], top_value])
    source_term = pressure_source
    smoothed = pressure_source
    for level_index in range(LEVELS):

        def operator(
            iterate, centre_coef=centre_coef, below_coef=below_coef, above_coef=above_coef
        ):
            return level_apply(iterate, centre_coef, below_coef, above_coef, bottom_flag)

        iterate = smooth_with(operator, source_term, centre_coef, below_coef, above_coef, SWEEPS)
        residual = source_term - operator(iterate)
        if level_index == 0:
            smoothed = iterate
        source_term = restrict(residual)
        centre_coef = 0.5 * (centre_coef[0::2] + centre_coef[1::2])
        below_coef = below_coef[0::2]
        above_coef = above_coef[1::2]
    columns = lax.all_gather(source_term, "gy", axis=1, tiled=True)
    slab_source, slab_centre, slab_below, slab_above = (
        lax.all_gather(columns, "gz", axis=2, tiled=True),
        lax.all_gather(centre_coef, "gz", axis=0, tiled=True),
        lax.all_gather(below_coef, "gz", axis=0, tiled=True),
        lax.all_gather(above_coef, "gz", axis=0, tiled=True),
    )

    def coarse_operator(iterate):
        return slab_apply(iterate, slab_centre, slab_below, slab_above)

    coarse_solution = smooth_with(
        coarse_operator, slab_source, slab_centre, slab_below, slab_above, COARSE_SWEEPS
    )
    return (smoothed, coarse_solution)


def solution(mesh):
    return jax.shard_map(
        on_device,
        mesh=mesh,
        in_specs=(P("gx", "gy", "gz"), P("gz"), P("gz")),
        out_specs=(P("gx", "gy", "gz"), P("gx", None, None)),
        check_vma=False,
    )
```

profile of v0, /device:TPU:57, one launch (start us, length us, event | category | flops | bytes accessed | tf_op | source)
XLA Modules:
  0.0 528.1 jit_solution(14697296491463403184)
XLA Ops:
  12.5 3.6 collective-permute-done.2
  28.5 4.5 fusion.78
  36.9 3.6 collective-permute-done.8
  52.1 4.4 fusion.63
  60.4 3.6 collective-permute-done.14
  76.2 4.2 fusion.48
  83.9 3.6 collective-permute-done.20
  99.3 4.5 fusion.33
  123.8 4.4 fusion.18
  148.0 4.4 fusion.3
  152.4 68.4 %reshape.50 = f32[8,2,32,2,128,2]{5,4,3,2,1,0:T(8,128)} reshape(f32[16,64,256]{2,1,0:T(8,128)S(1)} %fusion.3) | data formatting | bytes 2097152 | tf_op jit(solution)/shard_map/reshape | solution.py:86
  220.8 20.8 %reduce_sum.27 = f32[8,32,128]{2,1,0:T(8,128)S(1)} reduce(f32[8,2,32,2,128,2]{5,4,3,2,1,0:T(8,128)} %reshape.50, f32[]{:T(128)} %constant.14.clone.1), dimensions={1,3,5}, to_apply=%region_0.1 | reduce | flops 229376 | bytes 1179652 | tf_op jit(solution)/shard_map/reduce_sum | solution.py:87
  254.7 4.0 collective-permute-done.41
  272.0 3.9 collective-permute-done.47
  290.1 3.9 collective-permute-done.53
  307.6 4.2 collective-permute-done.59
  324.8 4.3 collective-permute-done.65
  341.9 3.9 collective-permute-done.71
  347.2 9.7 %reshape.51 = f32[4,2,16,2,64,2]{5,4,3,2,1,0:T(8,128)} reshape(f32[8,32,128]{2,1,0:T(8,128)S(1)} %fusion.91) | data formatting | bytes 262144 | tf_op jit(solution)/shard_map/reshape | solution.py:86
  357.0 4.0 reduce_sum.28
  451.8 6.4 %all-reduce.17 = (f32[128]{0:T(128)S(1)}, f32[128]{0:T(128)S(1)}, f32[128]{0:T(128)S(1)}) all-reduce(f32[128]{0:T(128)S(1)} %dynamic-update-slice.2, f32[128]{0:T(128)S(1)} %dynamic-update-slice.1, f32[128]{0:T(128)S(1)} %multiply_dynamic-update-slice_fusion), channel_id=1, replica_groups=mesh['gx'=8,'gy'=4,'gz'=4] {'gz'}, use_global_device_ids=true, to_apply=%add.16 | all-reduce | flops 384 | bytes 3072
  464.9 9.0 %all_gather.15 = f32[2,32,32]{2,0,1:T(2,128)S(1)} all-gather(f32[2,8,32]{2,0,1:T(2,128)S(1)} %copy.355), channel_id=1, replica_groups=mesh['gx'=8,'gy'=4,'gz'=4] {'gy'}, dimensions={1}, use_global_device_ids=true | all-gather | bytes 10240 | tf_op jit(solution)/shard_map/all_gather | solution.py:113
  474.0 12.1 %all_gather.16 = f32[2,32,128]{1,0,2:T(2,128)S(1)} all-gather(f32[2,32,32]{1,0,2:T(2,128)S(1)} %copy.356), channel_id=1, replica_groups=mesh['gx'=8,'gy'=4,'gz'=4] {'gz'}, dimensions={2}, use_global_device_ids=true | all-gather | bytes 40960 | tf_op jit(solution)/shard_map/all_gather | solution.py:115
  486.3 8.9 %collective-permute-start.109 = (f32[1,32,128]{2,1,0:T(8,128)S(1)}, f32[1,32,128]{2,1,0:T(8,128)S(1)}, u32[]{:S(2)}, u32[]{:S(2)}) collective-permute-start(f32[1,32,128]{2,1,0:T(8,128)S(1)} %get-tuple-element.167), channel_id=1, source_target_pairs={{112,0},{0,16},{16,32},{32,48},{48,64},{64,80},{80,96},{96,112},{1... | collective-permute-start | bytes 49160 | tf_op jit(solution)/shard_map/ppermute | solution.py:29
  (522 shorter events, 321.3 us)
Async XLA Ops:
  1.8 4.7 collective-permute-start
  11.2 4.9 collective-permute-start.2
  35.6 4.9 collective-permute-start.8
  59.1 4.9 collective-permute-start.14
  82.5 4.9 collective-permute-start.20
  106.1 4.9 collective-permute-start.26
  130.9 4.9 collective-permute-start.32
  252.4 6.2 %collective-permute-start.41 = (f32[10,34,1]{2,1,0:T(8,128)S(1)}, f32[10,34,1]{2,1,0:T(8,128)S(1)}, u32[]{:S(2)}, u32[]{:S(2)}) collective-permute-start(f32[10,34,1]{2,1,0:T(8,128)S(1)} %get-tuple-element.63), channel_id=1, source_target_pairs={{0,1},{1,2},{2,3},{3,0},{4,5},{5,6},{6,7},{7,4},{8,9},{9,10},{10,1... | collective-permute-start | bytes 4088 | tf_op jit(solution)/shard_map/ppermute | solution.py:18
  254.2 5.8 %collective-permute-start.42 = (f32[10,34,1]{2,1,0:T(8,128)S(1)}, f32[10,34,1]{2,1,0:T(8,128)S(1)}, u32[]{:S(2)}, u32[]{:S(2)}) collective-permute-start(f32[10,34,1]{2,1,0:T(8,128)S(1)} %get-tuple-element.64), channel_id=1, source_target_pairs={{1,0},{2,1},{3,2},{0,3},{5,4},{6,5},{7,6},{4,7},{9,8},{10,9},{11,1... | collective-permute-start | bytes 4088 | tf_op jit(solution)/shard_map/ppermute | solution.py:21
  270.3 5.7 %collective-permute-start.47 = (f32[10,34,1]{2,1,0:T(8,128)S(1)}, f32[10,34,1]{2,1,0:T(8,128)S(1)}, u32[]{:S(2)}, u32[]{:S(2)}) collective-permute-start(f32[10,34,1]{2,1,0:T(8,128)S(1)} %get-tuple-element.61), channel_id=1, source_target_pairs={{0,1},{1,2},{2,3},{3,0},{4,5},{5,6},{6,7},{7,4},{8,9},{9,10},{10,1... | collective-permute-start | bytes 4088 | tf_op jit(solution)/shard_map/ppermute | solution.py:18
  272.0 5.8 %collective-permute-start.48 = (f32[10,34,1]{2,1,0:T(8,128)S(1)}, f32[10,34,1]{2,1,0:T(8,128)S(1)}, u32[]{:S(2)}, u32[]{:S(2)}) collective-permute-start(f32[10,34,1]{2,1,0:T(8,128)S(1)} %get-tuple-element.62), channel_id=1, source_target_pairs={{1,0},{2,1},{3,2},{0,3},{5,4},{6,5},{7,6},{4,7},{9,8},{10,9},{11,1... | collective-permute-start | bytes 4088 | tf_op jit(solution)/shard_map/ppermute | solution.py:21
  288.3 5.7 %collective-permute-start.53 = (f32[10,34,1]{2,1,0:T(8,128)S(1)}, f32[10,34,1]{2,1,0:T(8,128)S(1)}, u32[]{:S(2)}, u32[]{:S(2)}) collective-permute-start(f32[10,34,1]{2,1,0:T(8,128)S(1)} %get-tuple-element.59), channel_id=1, source_target_pairs={{0,1},{1,2},{2,3},{3,0},{4,5},{5,6},{6,7},{7,4},{8,9},{9,10},{10,1... | collective-permute-start | bytes 4088 | tf_op jit(solution)/shard_map/ppermute | solution.py:18
  290.1 5.6 %collective-permute-start.54 = (f32[10,34,1]{2,1,0:T(8,128)S(1)}, f32[10,34,1]{2,1,0:T(8,128)S(1)}, u32[]{:S(2)}, u32[]{:S(2)}) collective-permute-start(f32[10,34,1]{2,1,0:T(8,128)S(1)} %get-tuple-element.60), channel_id=1, source_target_pairs={{1,0},{2,1},{3,2},{0,3},{5,4},{6,5},{7,6},{4,7},{9,8},{10,9},{11,1... | collective-permute-start | bytes 4088 | tf_op jit(solution)/shard_map/ppermute | solution.py:21
  305.9 5.9 %collective-permute-start.59 = (f32[10,34,1]{2,1,0:T(8,128)S(1)}, f32[10,34,1]{2,1,0:T(8,128)S(1)}, u32[]{:S(2)}, u32[]{:S(2)}) collective-permute-start(f32[10,34,1]{2,1,0:T(8,128)S(1)} %get-tuple-element.57), channel_id=1, source_target_pairs={{0,1},{1,2},{2,3},{3,0},{4,5},{5,6},{6,7},{7,4},{8,9},{9,10},{10,1... | collective-permute-start | bytes 4088 | tf_op jit(solution)/shard_map/ppermute | solution.py:18
  307.2 5.7 %collective-permute-start.60 = (f32[10,34,1]{2,1,0:T(8,128)S(1)}, f32[10,34,1]{2,1,0:T(8,128)S(1)}, u32[]{:S(2)}, u32[]{:S(2)}) collective-permute-start(f32[10,34,1]{2,1,0:T(8,128)S(1)} %get-tuple-element.58), channel_id=1, source_target_pairs={{1,0},{2,1},{3,2},{0,3},{5,4},{6,5},{7,6},{4,7},{9,8},{10,9},{11,1... | collective-permute-start | bytes 4088 | tf_op jit(solution)/shard_map/ppermute | solution.py:21
  323.3 5.9 %collective-permute-start.65 = (f32[10,34,1]{2,1,0:T(8,128)S(1)}, f32[10,34,1]{2,1,0:T(8,128)S(1)}, u32[]{:S(2)}, u32[]{:S(2)}) collective-permute-start(f32[10,34,1]{2,1,0:T(8,128)S(1)} %get-tuple-element.55), channel_id=1, source_target_pairs={{0,1},{1,2},{2,3},{3,0},{4,5},{5,6},{6,7},{7,4},{8,9},{9,10},{10,1... | collective-permute-start | bytes 4088 | tf_op jit(solution)/shard_map/ppermute | solution.py:18
  324.4 5.8 %collective-permute-start.66 = (f32[10,34,1]{2,1,0:T(8,128)S(1)}, f32[10,34,1]{2,1,0:T(8,128)S(1)}, u32[]{:S(2)}, u32[]{:S(2)}) collective-permute-start(f32[10,34,1]{2,1,0:T(8,128)S(1)} %get-tuple-element.56), channel_id=1, source_target_pairs={{1,0},{2,1},{3,2},{0,3},{5,4},{6,5},{7,6},{4,7},{9,8},{10,9},{11,1... | collective-permute-start | bytes 4088 | tf_op jit(solution)/shard_map/ppermute | solution.py:21
  340.4 5.4 %collective-permute-start.71 = (f32[10,34,1]{2,1,0:T(8,128)S(1)}, f32[10,34,1]{2,1,0:T(8,128)S(1)}, u32[]{:S(2)}, u32[]{:S(2)}) collective-permute-start(f32[10,34,1]{2,1,0:T(8,128)S(1)} %get-tuple-element.53), channel_id=1, source_target_pairs={{0,1},{1,2},{2,3},{3,0},{4,5},{5,6},{6,7},{7,4},{8,9},{9,10},{10,1... | collective-permute-start | bytes 4088 | tf_op jit(solution)/shard_map/ppermute | solution.py:18
  341.5 5.6 %collective-permute-start.72 = (f32[10,34,1]{2,1,0:T(8,128)S(1)}, f32[10,34,1]{2,1,0:T(8,128)S(1)}, u32[]{:S(2)}, u32[]{:S(2)}) collective-permute-start(f32[10,34,1]{2,1,0:T(8,128)S(1)} %get-tuple-element.54), channel_id=1, source_target_pairs={{1,0},{2,1},{3,2},{0,3},{5,4},{6,5},{7,6},{4,7},{9,8},{10,9},{11,1... | collective-permute-start | bytes 4088 | tf_op jit(solution)/shard_map/ppermute | solution.py:21
  441.4 4.8 collective-permute-start.103
  448.6 9.6 %collective-permute-start.105 = (f32[6,1,64]{2,1,0:T(1,128)S(1)}, f32[6,1,64]{2,1,0:T(1,128)S(1)}, u32[]{:S(2)}, u32[]{:S(2)}) collective-permute-start(f32[6,1,64]{2,1,0:T(1,128)S(1)} %get-tuple-element.101), channel_id=1, source_target_pairs={{0,4},{4,8},{8,12},{12,0},{1,5},{5,9},{9,13},{13,1},{2,6},{6,10},{... | collective-permute-start | bytes 4616 | tf_op jit(solution)/shard_map/ppermute | solution.py:18
  448.7 9.5 %collective-permute-start.106 = (f32[6,1,64]{2,1,0:T(1,128)S(1)}, f32[6,1,64]{2,1,0:T(1,128)S(1)}, u32[]{:S(2)}, u32[]{:S(2)}) collective-permute-start(f32[6,1,64]{2,1,0:T(1,128)S(1)} %get-tuple-element.102), channel_id=1, source_target_pairs={{4,0},{8,4},{12,8},{0,12},{5,1},{9,5},{13,9},{1,13},{6,2},{10,6},{... | collective-permute-start | bytes 4616 | tf_op jit(solution)/shard_map/ppermute | solution.py:21
  458.3 4.8 collective-permute-start.107
  486.3 9.7 %collective-permute-start.109 = (f32[1,32,128]{2,1,0:T(8,128)S(1)}, f32[1,32,128]{2,1,0:T(8,128)S(1)}, u32[]{:S(2)}, u32[]{:S(2)}) collective-permute-start(f32[1,32,128]{2,1,0:T(8,128)S(1)} %get-tuple-element.167), channel_id=1, source_target_pairs={{112,0},{0,16},{16,32},{32,48},{48,64},{64,80},{80,96},{96,112},{1... | collective-permute-start | bytes 49160 | tf_op jit(solution)/shard_map/ppermute | solution.py:29
  (139 other events, 673.2 us)
where the time goes:
time: 537 us; the launch traced here: 528 us
  waiting for transfers between devices  185 us (34%)
  starting transfers between devices  138 us (26%)
  local copies, waits for them, and re-layouts  115 us (21%)
  other arithmetic  60.4 us (11%)
  blocking collectives  27.5 us (5%)
    ppermute x54, starting transfers between devices, padded_2(): lax.ppermute(lax.slice_in_dim(block, block.shape[dim] - width, None, axis...  83.7 us
    ppermute x54, waiting for transfers between devices, padded_2(): lax.ppermute(lax.slice_in_dim(block, 0, width, axis=dim), axis, backward)  81.7 us
    reshape x3, local copies, waits for them, and re-layouts, restrict(): residual.reshape(extent[0] // 2, 2, extent[1] // 2, 2, extent[2] // 2, 2)  79.2 us
    ppermute x54, waiting for transfers between devices, padded_2(): lax.ppermute(lax.slice_in_dim(block, block.shape[dim] - width, None, axis...  73.4 us
    ppermute x54, starting transfers between devices, padded_2(): lax.ppermute(lax.slice_in_dim(block, 0, width, axis=dim), axis, backward)  40.1 us
    ppermute x14, waiting for transfers between devices, passed_along(): return lax.ppermute(block, axis, route)  27.7 us
    reduce_sum x3, other arithmetic, restrict(): return 0.5 * jnp.sum(blocks, axis=(1, 3, 5))  24.9 us
    add x22, other arithmetic, smooth_with(): iterate + damping * (source_term - operator(iterate)) * inverse_diag  24.8 us
  transfers between devices with their start and end apart: 123, of which 107 were waited for; matrix products, arithmetic and copies ran while one was open for 3% of the time, Pallas kernels for 0%

commit v1 on v0

--- a/solution.py
+++ b/solution.py
@@ -112,7 +112,9 @@
         above_coef = above_coef[1::2]
     columns = lax.all_gather(source_term, "gy", axis=1, tiled=True)
     slab_source, slab_centre, slab_below, slab_above = (
-        lax.all_gather(columns, "gz", axis=2, tiled=True),
+        jnp.concatenate(
+            lax.all_to_all(jnp.stack([columns] * lax.axis_size("gz")), "gz", 0, 0), axis=2
+        ),
         lax.all_gather(centre_coef, "gz", axis=0, tiled=True),
         lax.all_gather(below_coef, "gz", axis=0, tiled=True),
         lax.all_gather(above_coef, "gz", axis=0, tiled=True),

time: 537 us -> 534 us (level)
  blocking collectives: 27.5 us -> 16.6 us
    all_gather x1 -> x0, blocking collectives: 12.1 us -> none  [on_device(): lax.all_gather(columns, 'gz', axis=2, tiled=True)]
  transfers between devices with their start and end apart: 123 -> 124, of which waited for: 107 -> 107; matrix products, arithmetic and copies ran while one was open for 3% -> 3% of each run, Pallas kernels for 0% -> 0%
where the time goes in v1:
time: 534 us; the launch traced here: 523 us
  waiting for transfers between devices  185 us (35%)
  starting transfers between devices  141 us (26%)
  local copies, waits for them, and re-layouts  116 us (22%)
  other arithmetic  61.2 us (11%)
  blocking collectives  16.6 us (3%)
    ppermute x54, starting transfers between devices, padded_2(): lax.ppermute(lax.slice_in_dim(block, block.shape[dim] - width, None, axis...  84 us
    ppermute x54, waiting for transfers between devices, padded_2(): lax.ppermute(lax.slice_in_dim(block, 0, width, axis=dim), axis, backward)  81.3 us
    reshape x3, local copies, waits for them, and re-layouts, restrict(): residual.reshape(extent[0] // 2, 2, extent[1] // 2, 2, extent[2] // 2, 2)  79.2 us
    ppermute x54, waiting for transfers between devices, padded_2(): lax.ppermute(lax.slice_in_dim(block, block.shape[dim] - width, None, axis...  71.4 us
    ppermute x54, starting transfers between devices, padded_2(): lax.ppermute(lax.slice_in_dim(block, 0, width, axis=dim), axis, backward)  39.3 us
    ppermute x14, waiting for transfers between devices, passed_along(): return lax.ppermute(block, axis, route)  27.7 us
    reduce_sum x3, other arithmetic, restrict(): return 0.5 * jnp.sum(blocks, axis=(1, 3, 5))  24.9 us
    add x22, other arithmetic, smooth_with(): iterate + damping * (source_term - operator(iterate)) * inverse_diag  24.8 us
  transfers between devices with their start and end apart: 124, of which 107 were waited for; matrix products, arithmetic and copies ran while one was open for 3% of the time, Pallas kernels for 0%

profile of v1, /device:TPU:57, one launch (start us, length us, event | category | flops | bytes accessed | tf_op | source)
XLA Modules:
  0.0 523.1 jit_solution(3714311359645974238)
XLA Ops:
  12.6 3.6 collective-permute-done.2
  28.6 4.5 fusion.78
  37.0 3.6 collective-permute-done.8
  52.2 4.4 fusion.63
  60.5 3.6 collective-permute-done.14
  76.3 4.2 fusion.48
  83.9 3.6 collective-permute-done.20
  99.3 4.5 fusion.33
  123.9 4.4 fusion.18
  148.1 4.4 fusion.3
  152.5 68.4 %reshape.58 = f32[8,2,32,2,128,2]{5,4,3,2,1,0:T(8,128)} reshape(f32[16,64,256]{2,1,0:T(8,128)S(1)} %fusion.3) | data formatting | bytes 2097152 | tf_op jit(solution)/shard_map/reshape | solution.py:86
  220.9 20.8 %reduce_sum.27 = f32[8,32,128]{2,1,0:T(8,128)S(1)} reduce(f32[8,2,32,2,128,2]{5,4,3,2,1,0:T(8,128)} %reshape.58, f32[]{:T(128)} %constant.14.clone.1), dimensions={1,3,5}, to_apply=%region_0.1 | reduce | flops 229376 | bytes 1179652 | tf_op jit(solution)/shard_map/reduce_sum | solution.py:87
  254.8 4.0 collective-permute-done.41
  272.1 3.9 collective-permute-done.47
  290.2 3.9 collective-permute-done.53
  307.7 4.2 collective-permute-done.59
  324.9 4.3 collective-permute-done.65
  342.0 3.9 collective-permute-done.71
  347.3 9.7 %reshape.59 = f32[4,2,16,2,64,2]{5,4,3,2,1,0:T(8,128)} reshape(f32[8,32,128]{2,1,0:T(8,128)S(1)} %fusion.91) | data formatting | bytes 262144 | tf_op jit(solution)/shard_map/reshape | solution.py:86
  357.1 4.0 reduce_sum.28
  454.1 7.2 %all-reduce.17 = (f32[128]{0:T(128)S(1)}, f32[128]{0:T(128)S(1)}, f32[128]{0:T(128)S(1)}) all-reduce(f32[128]{0:T(128)S(1)} %dynamic-update-slice.2, f32[128]{0:T(128)S(1)} %dynamic-update-slice.1, f32[128]{0:T(128)S(1)} %multiply_dynamic-update-slice_fusion), channel_id=1, replica_groups=mesh['gx'=8,'gy'=4,'gz'=4] {'gz'}, use_global_device_ids=true, to_apply=%add.16 | all-reduce | flops 384 | bytes 3072
  462.7 9.4 %all_gather.12 = f32[2,32,32]{2,1,0:T(8,128)S(1)} all-gather(f32[2,8,32]{2,1,0:T(8,128)S(1)} %broadcast_multiply_fusion.4), channel_id=1, replica_groups=mesh['gx'=8,'gy'=4,'gz'=4] {'gy'}, dimensions={1}, use_global_device_ids=true | all-gather | bytes 10240 | tf_op jit(solution)/shard_map/all_gather | solution.py:113
  472.8 4.5 all-to-all-start
  482.1 8.1 %collective-permute-start.109 = (f32[1,32,128]{2,1,0:T(8,128)S(1)}, f32[1,32,128]{2,1,0:T(8,128)S(1)}, u32[]{:S(2)}, u32[]{:S(2)}) collective-permute-start(f32[1,32,128]{2,1,0:T(8,128)S(1)} %get-tuple-element.165), channel_id=1, source_target_pairs={{112,0},{0,16},{16,32},{32,48},{48,64},{64,80},{80,96},{96,112},{1... | collective-permute-start | bytes 49160 | tf_op jit(solution)/shard_map/ppermute | solution.py:29
  (527 shorter events, 323.5 us)
Async XLA Ops:
  1.8 4.5 collective-permute-start
  11.2 4.9 collective-permute-start.2
  35.7 4.9 collective-permute-start.8
  59.2 4.9 collective-permute-start.14
  82.6 4.9 collective-permute-start.20
  106.2 4.9 collective-permute-start.26
  131.0 4.9 collective-permute-start.32
  252.5 6.3 %collective-permute-start.41 = (f32[10,34,1]{2,1,0:T(8,128)S(1)}, f32[10,34,1]{2,1,0:T(8,128)S(1)}, u32[]{:S(2)}, u32[]{:S(2)}) collective-permute-start(f32[10,34,1]{2,1,0:T(8,128)S(1)} %get-tuple-element.61), channel_id=1, source_target_pairs={{0,1},{1,2},{2,3},{3,0},{4,5},{5,6},{6,7},{7,4},{8,9},{9,10},{10,1... | collective-permute-start | bytes 4088 | tf_op jit(solution)/shard_map/ppermute | solution.py:18
  254.3 5.8 %collective-permute-start.42 = (f32[10,34,1]{2,1,0:T(8,128)S(1)}, f32[10,34,1]{2,1,0:T(8,128)S(1)}, u32[]{:S(2)}, u32[]{:S(2)}) collective-permute-start(f32[10,34,1]{2,1,0:T(8,128)S(1)} %get-tuple-element.62), channel_id=1, source_target_pairs={{1,0},{2,1},{3,2},{0,3},{5,4},{6,5},{7,6},{4,7},{9,8},{10,9},{11,1... | collective-permute-start | bytes 4088 | tf_op jit(solution)/shard_map/ppermute | solution.py:21
  270.4 5.7 %collective-permute-start.47 = (f32[10,34,1]{2,1,0:T(8,128)S(1)}, f32[10,34,1]{2,1,0:T(8,128)S(1)}, u32[]{:S(2)}, u32[]{:S(2)}) collective-permute-start(f32[10,34,1]{2,1,0:T(8,128)S(1)} %get-tuple-element.59), channel_id=1, source_target_pairs={{0,1},{1,2},{2,3},{3,0},{4,5},{5,6},{6,7},{7,4},{8,9},{9,10},{10,1... | collective-permute-start | bytes 4088 | tf_op jit(solution)/shard_map/ppermute | solution.py:18
  272.1 5.8 %collective-permute-start.48 = (f32[10,34,1]{2,1,0:T(8,128)S(1)}, f32[10,34,1]{2,1,0:T(8,128)S(1)}, u32[]{:S(2)}, u32[]{:S(2)}) collective-permute-start(f32[10,34,1]{2,1,0:T(8,128)S(1)} %get-tuple-element.60), channel_id=1, source_target_pairs={{1,0},{2,1},{3,2},{0,3},{5,4},{6,5},{7,6},{4,7},{9,8},{10,9},{11,1... | collective-permute-start | bytes 4088 | tf_op jit(solution)/shard_map/ppermute | solution.py:21
  288.4 5.7 %collective-permute-start.53 = (f32[10,34,1]{2,1,0:T(8,128)S(1)}, f32[10,34,1]{2,1,0:T(8,128)S(1)}, u32[]{:S(2)}, u32[]{:S(2)}) collective-permute-start(f32[10,34,1]{2,1,0:T(8,128)S(1)} %get-tuple-element.57), channel_id=1, source_target_pairs={{0,1},{1,2},{2,3},{3,0},{4,5},{5,6},{6,7},{7,4},{8,9},{9,10},{10,1... | collective-permute-start | bytes 4088 | tf_op jit(solution)/shard_map/ppermute | solution.py:18
  290.2 5.6 %collective-permute-start.54 = (f32[10,34,1]{2,1,0:T(8,128)S(1)}, f32[10,34,1]{2,1,0:T(8,128)S(1)}, u32[]{:S(2)}, u32[]{:S(2)}) collective-permute-start(f32[10,34,1]{2,1,0:T(8,128)S(1)} %get-tuple-element.58), channel_id=1, source_target_pairs={{1,0},{2,1},{3,2},{0,3},{5,4},{6,5},{7,6},{4,7},{9,8},{10,9},{11,1... | collective-permute-start | bytes 4088 | tf_op jit(solution)/shard_map/ppermute | solution.py:21
  306.0 5.9 %collective-permute-start.59 = (f32[10,34,1]{2,1,0:T(8,128)S(1)}, f32[10,34,1]{2,1,0:T(8,128)S(1)}, u32[]{:S(2)}, u32[]{:S(2)}) collective-permute-start(f32[10,34,1]{2,1,0:T(8,128)S(1)} %get-tuple-element.55), channel_id=1, source_target_pairs={{0,1},{1,2},{2,3},{3,0},{4,5},{5,6},{6,7},{7,4},{8,9},{9,10},{10,1... | collective-permute-start | bytes 4088 | tf_op jit(solution)/shard_map/ppermute | solution.py:18
  307.3 5.7 %collective-permute-start.60 = (f32[10,34,1]{2,1,0:T(8,128)S(1)}, f32[10,34,1]{2,1,0:T(8,128)S(1)}, u32[]{:S(2)}, u32[]{:S(2)}) collective-permute-start(f32[10,34,1]{2,1,0:T(8,128)S(1)} %get-tuple-element.56), channel_id=1, source_target_pairs={{1,0},{2,1},{3,2},{0,3},{5,4},{6,5},{7,6},{4,7},{9,8},{10,9},{11,1... | collective-permute-start | bytes 4088 | tf_op jit(solution)/shard_map/ppermute | solution.py:21
  323.4 5.9 %collective-permute-start.65 = (f32[10,34,1]{2,1,0:T(8,128)S(1)}, f32[10,34,1]{2,1,0:T(8,128)S(1)}, u32[]{:S(2)}, u32[]{:S(2)}) collective-permute-start(f32[10,34,1]{2,1,0:T(8,128)S(1)} %get-tuple-element.53), channel_id=1, source_target_pairs={{0,1},{1,2},{2,3},{3,0},{4,5},{5,6},{6,7},{7,4},{8,9},{9,10},{10,1... | collective-permute-start | bytes 4088 | tf_op jit(solution)/shard_map/ppermute | solution.py:18
  324.4 5.8 %collective-permute-start.66 = (f32[10,34,1]{2,1,0:T(8,128)S(1)}, f32[10,34,1]{2,1,0:T(8,128)S(1)}, u32[]{:S(2)}, u32[]{:S(2)}) collective-permute-start(f32[10,34,1]{2,1,0:T(8,128)S(1)} %get-tuple-element.54), channel_id=1, source_target_pairs={{1,0},{2,1},{3,2},{0,3},{5,4},{6,5},{7,6},{4,7},{9,8},{10,9},{11,1... | collective-permute-start | bytes 4088 | tf_op jit(solution)/shard_map/ppermute | solution.py:21
  340.5 5.4 %collective-permute-start.71 = (f32[10,34,1]{2,1,0:T(8,128)S(1)}, f32[10,34,1]{2,1,0:T(8,128)S(1)}, u32[]{:S(2)}, u32[]{:S(2)}) collective-permute-start(f32[10,34,1]{2,1,0:T(8,128)S(1)} %get-tuple-element.51), channel_id=1, source_target_pairs={{0,1},{1,2},{2,3},{3,0},{4,5},{5,6},{6,7},{7,4},{8,9},{9,10},{10,1... | collective-permute-start | bytes 4088 | tf_op jit(solution)/shard_map/ppermute | solution.py:18
  341.5 5.6 %collective-permute-start.72 = (f32[10,34,1]{2,1,0:T(8,128)S(1)}, f32[10,34,1]{2,1,0:T(8,128)S(1)}, u32[]{:S(2)}, u32[]{:S(2)}) collective-permute-start(f32[10,34,1]{2,1,0:T(8,128)S(1)} %get-tuple-element.52), channel_id=1, source_target_pairs={{1,0},{2,1},{3,2},{0,3},{5,4},{6,5},{7,6},{4,7},{9,8},{10,9},{11,1... | collective-permute-start | bytes 4088 | tf_op jit(solution)/shard_map/ppermute | solution.py:21
  441.5 4.8 collective-permute-start.103
  452.6 8.7 %collective-permute-start.107 = (f32[6,18,1]{2,1,0:T(8,128)S(1)}, f32[6,18,1]{2,1,0:T(8,128)S(1)}, u32[]{:S(2)}, u32[]{:S(2)}) collective-permute-start(f32[6,18,1]{2,1,0:T(8,128)S(1)} %get-tuple-element.87), channel_id=1, source_target_pairs={{0,1},{1,2},{2,3},{3,0},{4,5},{5,6},{6,7},{7,4},{8,9},{9,10},{10,1... | collective-permute-start | bytes 1304 | tf_op jit(solution)/shard_map/ppermute | solution.py:18
  453.7 7.7 %collective-permute-start.108 = (f32[6,18,1]{2,1,0:T(8,128)S(1)}, f32[6,18,1]{2,1,0:T(8,128)S(1)}, u32[]{:S(2)}, u32[]{:S(2)}) collective-permute-start(f32[6,18,1]{2,1,0:T(8,128)S(1)} %get-tuple-element.88), channel_id=1, source_target_pairs={{1,0},{2,1},{3,2},{0,3},{5,4},{6,5},{7,6},{4,7},{9,8},{10,9},{11,1... | collective-permute-start | bytes 1304 | tf_op jit(solution)/shard_map/ppermute | solution.py:21
  472.8 7.6 %all-to-all-start = ((f32[4,1,2048]{2,1,0:T(1,128)}), f32[4,1,2048]{2,1,0:T(1,128)S(1)}, u32[]{:S(2)}, u32[]{:S(2)}) async-start(f32[4,1,2048]{2,1,0:T(1,128)} %reshape.78), calls=%async_computation | async-start | bytes 65536 | tf_op jit(solution)/shard_map/all_to_all | solution.py:116
  482.1 9.0 %collective-permute-start.109 = (f32[1,32,128]{2,1,0:T(8,128)S(1)}, f32[1,32,128]{2,1,0:T(8,128)S(1)}, u32[]{:S(2)}, u32[]{:S(2)}) collective-permute-start(f32[1,32,128]{2,1,0:T(8,128)S(1)} %get-tuple-element.165), channel_id=1, source_target_pairs={{112,0},{0,16},{16,32},{32,48},{48,64},{64,80},{80,96},{96,112},{1... | collective-permute-start | bytes 49160 | tf_op jit(solution)/shard_map/ppermute | solution.py:29
  (140 other events, 677.2 us)
